TPU v7x, 256 devices: a whole 4x4x8 slice. The times are simulated.
256 devices in a mesh: gx: 8 (over z_hi, core), gy: 8 (over z_lo, y), gz: 4 (over x).
Axes of the slice: x: 4, y: 4, z: 8 (z_hi: 4, z_lo: 2; z = z_hi * 2 + z_lo), core: 2. Of those that a mesh axis runs over, the one named last changes fastest.
Arguments:
- blocks: bfloat16 [16, 8, 8, 27, 128, 128], P('gx', 'gy', 'gz')
- pattern: int32 [16, 8, 8, 27], P('gx', 'gy'), may hold values 0 or 1
- order: int32 [16, 8, 8], P('gx', 'gy'), may hold values from 0 to 7, each once within a row
- start: float32 [16, 8, 8, 128], P('gx', 'gy', 'gz'), may hold values from -6 to 6
- rhs: float32 [16, 8, 8, 128], P('gx', 'gy', 'gz'), may hold values from -6 to 6
Outputs:
- smoothed: float32 [16, 8, 8, 128], P('gx', 'gy', 'gz')
- remainder: float32 [16, 8, 8, 128], P('gx', 'gy', 'gz')
Inputs may be any that keep to these rules, and one draw needn't show every extreme that they name: `order`: in every grid column the 8 slots name each plane exactly once. `pattern`: entry 13 is ignored.
All inputs are finite; a program needn't handle non-finite values. No bound on the sum of `pattern` on one device may be relied on, other than what follows from the above.
Results may differ from a plain program's by a relative error of at most 0.0081.
Values may be sent and summed in bfloat16 or wider, within the bound.
A program may use at most 64 MiB of HBM per device.

v0:
```python
import jax
import jax.numpy as jnp
from jax import lax
from jax.sharding import PartitionSpec as P

DEG = 4


def padded_2(cells, sides, width):
    for axis, dim in sides:
        count = lax.axis_size(axis)
        ends = count - 1
        head = lax.slice_in_dim(cells, 0, width, axis=dim)
        tail = lax.slice_in_dim(cells, cells.shape[dim] - width, cells.shape[dim], axis=dim)
        cells = jnp.concatenate(
            [
                lax.ppermute(tail, axis, [(i, (i + 1) % count) for i in range(ends)]),
                cells,
                lax.ppermute(head, axis, [((i + 1) % count, i) for i in range(ends)]),
            ],
            axis=dim,
        )
    return cells


def coupled_product(matrix, planes, rows, present):
    padded = padded_2(planes, (("gx", 0), ("gy", 1)), 1)
    padded = jnp.pad(padded, ((0, 0), (0, 0), (1, 1), (0, 0)))
    span_x, span_y = (planes.shape[0], planes.shape[1])
    height = padded.shape[2]
    keeping = jnp.where(jnp.arange(27) == 13, 1, present).astype(jnp.float32)
    offsets = jnp.arange(3, dtype=jnp.int32)
    places = jnp.arange(height, dtype=jnp.int32)
    target = rows[..., None, None] + offsets[:, None]
    select = (target == places).astype(jnp.float32)
    pieces = []
    for step_a in range(3):
        for step_b in range(3):
            column = padded[step_a : step_a + span_x, step_b : step_b + span_y]
            first = 9 * step_a + 3 * step_b
            table = (select * keeping[..., first : first + 3, None]).astype(jnp.bfloat16)
            picked = jnp.einsum(
                "xyscp,xypw->xyscw", table, column, preferred_element_type=jnp.float32
            )
            pieces.append(picked.astype(jnp.bfloat16))
    gathered = jnp.stack(pieces, axis=3)
    gathered = gathered.reshape(gathered.shape[:3] + (27, gathered.shape[-1]))
    return jnp.einsum("xysoj,xysoij->xysi", gathered, matrix, preferred_element_type=jnp.float32)


def by_plane(vector, order):
    places = jnp.arange(order.shape[2], dtype=jnp.int32)
    table = (order[..., None] == places).astype(jnp.bfloat16)
    moved = jnp.einsum("xysp,xysw->xypw", table, vector, preferred_element_type=jnp.float32)
    return moved.astype(jnp.bfloat16)


def local(blocks, pattern, order, start, rhs):
    depth = blocks.shape[2]
    first = lax.axis_index("gz") * depth
    smoothed, target = (start, rhs)
    rows = lax.dynamic_slice_in_dim(order, first, depth, 2)
    present = lax.dynamic_slice_in_dim(pattern, first, depth, 2)

    def operator(vector):
        column = lax.all_gather(vector.astype(jnp.bfloat16), "gz", axis=2, tiled=True)
        planes = by_plane(column, order)
        return coupled_product(blocks, planes, rows, present)

    center = 1.0
    spread = 0.8
    sigma = center / spread
    rho = 1.0 / sigma
    remainder = target - operator(smoothed)
    search = remainder / center
    for number in range(DEG):
        smoothed = smoothed + search
        remainder = remainder - operator(search)
        if number + 1 < DEG:
            following = 1.0 / (2.0 * sigma - rho)
            search = following * rho * search + 2.0 * following / spread * remainder
            rho = following
    return (smoothed, remainder)


def solution(mesh):
    in_specs = (
        P("gx", "gy", "gz", None, None, None),
        P("gx", "gy", None, None),
        P("gx", "gy", None),
        P("gx", "gy", "gz", None),
        P("gx", "gy", "gz", None),
    )
    out_specs = (P("gx", "gy", "gz", None), P("gx", "gy", "gz", None))
    return jax.shard_map(local, mesh=mesh, in_specs=in_specs, out_specs=out_specs, check_vma=False)
```

profile of v0, /device:TPU:97, one launch (start us, length us, event | category | flops | bytes accessed | tf_op | source)
XLA Modules:
  0.0 160.3 jit_solution(5242034563477572541)
XLA Ops:
  0.7 0.8 copy.155
  1.5 7.8 %all_gather.15 = bf16[2,1,8,128]{3,0,1,2:T(2,128)(2,1)S(1)} all-gather(bf16[2,1,2,128]{3,0,1,2:T(2,128)(2,1)S(1)} %copy.155), channel_id=1, replica_groups=mesh['gx'=8,'gy'=8,'gz'=4] {'gz'}, dimensions={2}, use_global_device_ids=true | all-gather | bytes 5120 | tf_op jit(solution)/shard_map/all_gather | solution.py:66
  9.3 0.8 convolution_convert_fusion.49
  10.1 0.6 slice_bitcast_fusion.107
  10.7 7.8 %collective-permute-start = (bf16[1,1,8,128]{3,2,0,1:T(8,128)(2,1)}, bf16[1,1,8,128]{3,2,0,1:T(8,128)(2,1)S(1)}, u32[]{:S(2)}, u32[]{:S(2)}) collective-permute-start(bf16[1,1,8,128]{3,2,0,1:T(8,128)(2,1)} %get-tuple-element.24), channel_id=1, source_target_pairs={{0,32},{32,64},{64,96},{96,128},{128,160},{160,192},{192,224},{1,3... | collective-permute-start | bytes 6152 | tf_op jit(solution)/shard_map/ppermute | solution.py:17
  18.5 1.9 %collective-permute-start.1 = (bf16[1,1,8,128]{3,2,1,0:T(8,128)(2,1)}, bf16[1,1,8,128]{3,2,1,0:T(8,128)(2,1)S(1)}, u32[]{:S(2)}, u32[]{:S(2)}) collective-permute-start(bf16[1,1,8,128]{3,2,1,0:T(8,128)(2,1)} %get-tuple-element.25), channel_id=1, source_target_pairs={{32,0},{64,32},{96,64},{128,96},{160,128},{192,160},{224,192},{33,... | collective-permute-start | bytes 6152 | tf_op jit(solution)/shard_map/ppermute | solution.py:19
  20.4 0.6 iota_compare_fusion.9
  21.0 0.7 select_convert_fusion.54
  21.8 0.8 constant_dynamic-slice_fusion
  22.6 3.1 %collective-permute-done.1 = bf16[1,1,8,128]{3,2,1,0:T(8,128)(2,1)S(1)} collective-permute-done((bf16[1,1,8,128]{3,2,1,0:T(8,128)(2,1)}, bf16[1,1,8,128]{3,2,1,0:T(8,128)(2,1)S(1)}, u32[]{:S(2)}, u32[]{:S(2)}) %collective-permute-start.1) | collective-permute-done | bytes 2080 | tf_op jit(solution)/shard_map/ppermute | solution.py:19
  25.7 5.1 %collective-permute-start.3 = (bf16[4,1,8,128]{3,2,0,1:T(8,128)(2,1)S(1)}, bf16[4,1,8,128]{3,2,0,1:T(8,128)(2,1)S(1)}, u32[]{:S(2)}, u32[]{:S(2)}) collective-permute-start(bf16[4,1,8,128]{3,2,0,1:T(8,128)(2,1)S(1)} %pad_maximum_fusion), channel_id=1, source_target_pairs={{4,0},{8,4},{12,8},{16,12},{20,16},{24,20},{28,24},{5,1},{9,5},{13... | collective-permute-start | bytes 24584 | tf_op jit(solution)/shard_map/ppermute | solution.py:19
  30.8 1.9 %collective-permute-start.2 = (bf16[4,1,8,128]{3,2,0,1:T(8,128)(2,1)S(1)}, bf16[4,1,8,128]{3,2,0,1:T(8,128)(2,1)S(1)}, u32[]{:S(2)}, u32[]{:S(2)}) collective-permute-start(bf16[4,1,8,128]{3,2,0,1:T(8,128)(2,1)S(1)} %pad_maximum_fusion), channel_id=1, source_target_pairs={{0,4},{4,8},{8,12},{12,16},{16,20},{20,24},{24,28},{1,5},{5,9},{9,... | collective-permute-start | bytes 24584 | tf_op jit(solution)/shard_map/ppermute | solution.py:17
  32.8 4.5 %collective-permute-done.2 = bf16[4,1,8,128]{3,2,0,1:T(8,128)(2,1)S(1)} collective-permute-done((bf16[4,1,8,128]{3,2,0,1:T(8,128)(2,1)S(1)}, bf16[4,1,8,128]{3,2,0,1:T(8,128)(2,1)S(1)}, u32[]{:S(2)}, u32[]{:S(2)}) %collective-permute-start.2) | collective-permute-done | bytes 8224 | tf_op jit(solution)/shard_map/ppermute | solution.py:17
  39.2 1.0 fusion.8
  40.3 5.3 %all_gather.16 = bf16[2,1,8,128]{3,0,1,2:T(2,128)(2,1)S(1)} all-gather(bf16[2,1,2,128]{3,0,1,2:T(2,128)(2,1)S(1)} %get-tuple-element.12), channel_id=1, replica_groups=mesh['gx'=8,'gy'=8,'gz'=4] {'gz'}, dimensions={2}, use_global_device_ids=true | all-gather | bytes 5120 | tf_op jit(solution)/shard_map/all_gather | solution.py:66
  45.7 5.8 %collective-permute-start.4 = (bf16[1,1,8,128]{3,2,0,1:T(8,128)(2,1)S(1)}, bf16[1,1,8,128]{3,2,0,1:T(8,128)(2,1)S(1)}, u32[]{:S(2)}, u32[]{:S(2)}) collective-permute-start(bf16[1,1,8,128]{3,2,0,1:T(8,128)(2,1)S(1)} %get-tuple-element.22), channel_id=1, source_target_pairs={{0,32},{32,64},{64,96},{96,128},{128,160},{160,192},{192,224},{1,3... | collective-permute-start | bytes 6152 | tf_op jit(solution)/shard_map/ppermute | solution.py:17
  51.4 1.9 %collective-permute-start.5 = (bf16[1,1,8,128]{3,2,1,0:T(8,128)(2,1)S(1)}, bf16[1,1,8,128]{3,2,1,0:T(8,128)(2,1)S(1)}, u32[]{:S(2)}, u32[]{:S(2)}) collective-permute-start(bf16[1,1,8,128]{3,2,1,0:T(8,128)(2,1)S(1)} %get-tuple-element.23), channel_id=1, source_target_pairs={{32,0},{64,32},{96,64},{128,96},{160,128},{192,160},{224,192},{33,... | collective-permute-start | bytes 6152 | tf_op jit(solution)/shard_map/ppermute | solution.py:19
  53.4 5.1 %collective-permute-done.5 = bf16[1,1,8,128]{3,2,1,0:T(8,128)(2,1)S(1)} collective-permute-done((bf16[1,1,8,128]{3,2,1,0:T(8,128)(2,1)S(1)}, bf16[1,1,8,128]{3,2,1,0:T(8,128)(2,1)S(1)}, u32[]{:S(2)}, u32[]{:S(2)}) %collective-permute-start.5) | collective-permute-done | bytes 2080 | tf_op jit(solution)/shard_map/ppermute | solution.py:19
  58.5 1.9 %collective-permute-start.7 = (bf16[4,1,8,128]{3,2,0,1:T(8,128)(2,1)S(1)}, bf16[4,1,8,128]{3,2,0,1:T(8,128)(2,1)S(1)}, u32[]{:S(2)}, u32[]{:S(2)}) collective-permute-start(bf16[4,1,8,128]{3,2,0,1:T(8,128)(2,1)S(1)} %pad_maximum_fusion.1), channel_id=1, source_target_pairs={{4,0},{8,4},{12,8},{16,12},{20,16},{24,20},{28,24},{5,1},{9,5},{13... | collective-permute-start | bytes 24584 | tf_op jit(solution)/shard_map/ppermute | solution.py:19
  60.4 3.4 %collective-permute-start.6 = (bf16[4,1,8,128]{3,2,0,1:T(8,128)(2,1)S(1)}, bf16[4,1,8,128]{3,2,0,1:T(8,128)(2,1)S(1)}, u32[]{:S(2)}, u32[]{:S(2)}) collective-permute-start(bf16[4,1,8,128]{3,2,0,1:T(8,128)(2,1)S(1)} %pad_maximum_fusion.1), channel_id=1, source_target_pairs={{0,4},{4,8},{8,12},{12,16},{16,20},{20,24},{24,28},{1,5},{5,9},{9,... | collective-permute-start | bytes 24584 | tf_op jit(solution)/shard_map/ppermute | solution.py:17
  63.8 3.1 %collective-permute-done.6 = bf16[4,1,8,128]{3,2,0,1:T(8,128)(2,1)S(1)} collective-permute-done((bf16[4,1,8,128]{3,2,0,1:T(8,128)(2,1)S(1)}, bf16[4,1,8,128]{3,2,0,1:T(8,128)(2,1)S(1)}, u32[]{:S(2)}, u32[]{:S(2)}) %collective-permute-start.6) | collective-permute-done | bytes 8224 | tf_op jit(solution)/shard_map/ppermute | solution.py:17
  68.8 1.0 fusion.6
  69.8 7.0 %all_gather.17 = bf16[2,1,8,128]{3,0,1,2:T(2,128)(2,1)S(1)} all-gather(bf16[2,1,2,128]{3,0,1,2:T(2,128)(2,1)S(1)} %get-tuple-element.10), channel_id=1, replica_groups=mesh['gx'=8,'gy'=8,'gz'=4] {'gz'}, dimensions={2}, use_global_device_ids=true | all-gather | bytes 5120 | tf_op jit(solution)/shard_map/all_gather | solution.py:66
  76.9 5.1 %collective-permute-start.8 = (bf16[1,1,8,128]{3,2,0,1:T(8,128)(2,1)S(1)}, bf16[1,1,8,128]{3,2,0,1:T(8,128)(2,1)S(1)}, u32[]{:S(2)}, u32[]{:S(2)}) collective-permute-start(bf16[1,1,8,128]{3,2,0,1:T(8,128)(2,1)S(1)} %get-tuple-element.20), channel_id=1, source_target_pairs={{0,32},{32,64},{64,96},{96,128},{128,160},{160,192},{192,224},{1,3... | collective-permute-start | bytes 6152 | tf_op jit(solution)/shard_map/ppermute | solution.py:17
  82.1 1.9 %collective-permute-start.9 = (bf16[1,1,8,128]{3,2,1,0:T(8,128)(2,1)S(1)}, bf16[1,1,8,128]{3,2,1,0:T(8,128)(2,1)S(1)}, u32[]{:S(2)}, u32[]{:S(2)}) collective-permute-start(bf16[1,1,8,128]{3,2,1,0:T(8,128)(2,1)S(1)} %get-tuple-element.21), channel_id=1, source_target_pairs={{32,0},{64,32},{96,64},{128,96},{160,128},{192,160},{224,192},{33,... | collective-permute-start | bytes 6152 | tf_op jit(solution)/shard_map/ppermute | solution.py:19
  84.0 5.1 %collective-permute-done.9 = bf16[1,1,8,128]{3,2,1,0:T(8,128)(2,1)S(1)} collective-permute-done((bf16[1,1,8,128]{3,2,1,0:T(8,128)(2,1)S(1)}, bf16[1,1,8,128]{3,2,1,0:T(8,128)(2,1)S(1)}, u32[]{:S(2)}, u32[]{:S(2)}) %collective-permute-start.9) | collective-permute-done | bytes 2080 | tf_op jit(solution)/shard_map/ppermute | solution.py:19
  89.1 1.9 %collective-permute-start.11 = (bf16[4,1,8,128]{3,2,0,1:T(8,128)(2,1)S(1)}, bf16[4,1,8,128]{3,2,0,1:T(8,128)(2,1)S(1)}, u32[]{:S(2)}, u32[]{:S(2)}) collective-permute-start(bf16[4,1,8,128]{3,2,0,1:T(8,128)(2,1)S(1)} %pad_maximum_fusion.2), channel_id=1, source_target_pairs={{4,0},{8,4},{12,8},{16,12},{20,16},{24,20},{28,24},{5,1},{9,5},{13... | collective-permute-start | bytes 24584 | tf_op jit(solution)/shard_map/ppermute | solution.py:19
  91.0 3.4 %collective-permute-start.10 = (bf16[4,1,8,128]{3,2,0,1:T(8,128)(2,1)S(1)}, bf16[4,1,8,128]{3,2,0,1:T(8,128)(2,1)S(1)}, u32[]{:S(2)}, u32[]{:S(2)}) collective-permute-start(bf16[4,1,8,128]{3,2,0,1:T(8,128)(2,1)S(1)} %pad_maximum_fusion.2), channel_id=1, source_target_pairs={{0,4},{4,8},{8,12},{12,16},{16,20},{20,24},{24,28},{1,5},{5,9},{9,... | collective-permute-start | bytes 24584 | tf_op jit(solution)/shard_map/ppermute | solution.py:17
  94.4 3.1 %collective-permute-done.10 = bf16[4,1,8,128]{3,2,0,1:T(8,128)(2,1)S(1)} collective-permute-done((bf16[4,1,8,128]{3,2,0,1:T(8,128)(2,1)S(1)}, bf16[4,1,8,128]{3,2,0,1:T(8,128)(2,1)S(1)}, u32[]{:S(2)}, u32[]{:S(2)}) %collective-permute-start.10) | collective-permute-done | bytes 8224 | tf_op jit(solution)/shard_map/ppermute | solution.py:17
  99.4 1.0 fusion.4
  100.5 5.3 %all_gather.18 = bf16[2,1,8,128]{3,0,1,2:T(2,128)(2,1)S(1)} all-gather(bf16[2,1,2,128]{3,0,1,2:T(2,128)(2,1)S(1)} %get-tuple-element.8), channel_id=1, replica_groups=mesh['gx'=8,'gy'=8,'gz'=4] {'gz'}, dimensions={2}, use_global_device_ids=true | all-gather | bytes 5120 | tf_op jit(solution)/shard_map/all_gather | solution.py:66
  105.8 4.8 %collective-permute-start.12 = (bf16[1,1,8,128]{3,2,0,1:T(8,128)(2,1)S(1)}, bf16[1,1,8,128]{3,2,0,1:T(8,128)(2,1)S(1)}, u32[]{:S(2)}, u32[]{:S(2)}) collective-permute-start(bf16[1,1,8,128]{3,2,0,1:T(8,128)(2,1)S(1)} %get-tuple-element.18), channel_id=1, source_target_pairs={{0,32},{32,64},{64,96},{96,128},{128,160},{160,192},{192,224},{1,3... | collective-permute-start | bytes 6152 | tf_op jit(solution)/shard_map/ppermute | solution.py:17
  110.7 1.9 %collective-permute-start.13 = (bf16[1,1,8,128]{3,2,1,0:T(8,128)(2,1)S(1)}, bf16[1,1,8,128]{3,2,1,0:T(8,128)(2,1)S(1)}, u32[]{:S(2)}, u32[]{:S(2)}) collective-permute-start(bf16[1,1,8,128]{3,2,1,0:T(8,128)(2,1)S(1)} %get-tuple-element.19), channel_id=1, source_target_pairs={{32,0},{64,32},{96,64},{128,96},{160,128},{192,160},{224,192},{33,... | collective-permute-start | bytes 6152 | tf_op jit(solution)/shard_map/ppermute | solution.py:19
  112.6 5.1 %collective-permute-done.13 = bf16[1,1,8,128]{3,2,1,0:T(8,128)(2,1)S(1)} collective-permute-done((bf16[1,1,8,128]{3,2,1,0:T(8,128)(2,1)S(1)}, bf16[1,1,8,128]{3,2,1,0:T(8,128)(2,1)S(1)}, u32[]{:S(2)}, u32[]{:S(2)}) %collective-permute-start.13) | collective-permute-done | bytes 2080 | tf_op jit(solution)/shard_map/ppermute | solution.py:19
  117.7 1.9 %collective-permute-start.15 = (bf16[4,1,8,128]{3,2,0,1:T(8,128)(2,1)S(1)}, bf16[4,1,8,128]{3,2,0,1:T(8,128)(2,1)S(1)}, u32[]{:S(2)}, u32[]{:S(2)}) collective-permute-start(bf16[4,1,8,128]{3,2,0,1:T(8,128)(2,1)S(1)} %pad_maximum_fusion.3), channel_id=1, source_target_pairs={{4,0},{8,4},{12,8},{16,12},{20,16},{24,20},{28,24},{5,1},{9,5},{13... | collective-permute-start | bytes 24584 | tf_op jit(solution)/shard_map/ppermute | solution.py:19
  119.6 3.4 %collective-permute-start.14 = (bf16[4,1,8,128]{3,2,0,1:T(8,128)(2,1)S(1)}, bf16[4,1,8,128]{3,2,0,1:T(8,128)(2,1)S(1)}, u32[]{:S(2)}, u32[]{:S(2)}) collective-permute-start(bf16[4,1,8,128]{3,2,0,1:T(8,128)(2,1)S(1)} %pad_maximum_fusion.3), channel_id=1, source_target_pairs={{0,4},{4,8},{8,12},{12,16},{16,20},{20,24},{24,28},{1,5},{5,9},{9,... | collective-permute-start | bytes 24584 | tf_op jit(solution)/shard_map/ppermute | solution.py:17
  123.0 3.1 %collective-permute-done.14 = bf16[4,1,8,128]{3,2,0,1:T(8,128)(2,1)S(1)} collective-permute-done((bf16[4,1,8,128]{3,2,0,1:T(8,128)(2,1)S(1)}, bf16[4,1,8,128]{3,2,0,1:T(8,128)(2,1)S(1)}, u32[]{:S(2)}, u32[]{:S(2)}) %collective-permute-start.14) | collective-permute-done | bytes 8224 | tf_op jit(solution)/shard_map/ppermute | solution.py:17
  128.0 1.0 fusion.2
  129.1 7.0 %all_gather.19 = bf16[2,1,8,128]{3,0,1,2:T(2,128)(2,1)S(1)} all-gather(bf16[2,1,2,128]{3,0,1,2:T(2,128)(2,1)S(1)} %get-tuple-element.14), channel_id=1, replica_groups=mesh['gx'=8,'gy'=8,'gz'=4] {'gz'}, dimensions={2}, use_global_device_ids=true | all-gather | bytes 5120 | tf_op jit(solution)/shard_map/all_gather | solution.py:66
  136.2 5.1 %collective-permute-start.16 = (bf16[1,1,8,128]{3,2,0,1:T(8,128)(2,1)S(1)}, bf16[1,1,8,128]{3,2,0,1:T(8,128)(2,1)S(1)}, u32[]{:S(2)}, u32[]{:S(2)}) collective-permute-start(bf16[1,1,8,128]{3,2,0,1:T(8,128)(2,1)S(1)} %get-tuple-element.16), channel_id=1, source_target_pairs={{0,32},{32,64},{64,96},{96,128},{128,160},{160,192},{192,224},{1,3... | collective-permute-start | bytes 6152 | tf_op jit(solution)/shard_map/ppermute | solution.py:17
  141.3 1.9 %collective-permute-start.17 = (bf16[1,1,8,128]{3,2,1,0:T(8,128)(2,1)S(1)}, bf16[1,1,8,128]{3,2,1,0:T(8,128)(2,1)S(1)}, u32[]{:S(2)}, u32[]{:S(2)}) collective-permute-start(bf16[1,1,8,128]{3,2,1,0:T(8,128)(2,1)S(1)} %get-tuple-element.17), channel_id=1, source_target_pairs={{32,0},{64,32},{96,64},{128,96},{160,128},{192,160},{224,192},{33,... | collective-permute-start | bytes 6152 | tf_op jit(solution)/shard_map/ppermute | solution.py:19
  143.2 5.1 %collective-permute-done.17 = bf16[1,1,8,128]{3,2,1,0:T(8,128)(2,1)S(1)} collective-permute-done((bf16[1,1,8,128]{3,2,1,0:T(8,128)(2,1)S(1)}, bf16[1,1,8,128]{3,2,1,0:T(8,128)(2,1)S(1)}, u32[]{:S(2)}, u32[]{:S(2)}) %collective-permute-start.17) | collective-permute-done | bytes 2080 | tf_op jit(solution)/shard_map/ppermute | solution.py:19
  148.3 1.9 %collective-permute-start.19 = (bf16[4,1,8,128]{3,2,0,1:T(8,128)(2,1)S(1)}, bf16[4,1,8,128]{3,2,0,1:T(8,128)(2,1)S(1)}, u32[]{:S(2)}, u32[]{:S(2)}) collective-permute-start(bf16[4,1,8,128]{3,2,0,1:T(8,128)(2,1)S(1)} %pad_maximum_fusion.4), channel_id=1, source_target_pairs={{4,0},{8,4},{12,8},{16,12},{20,16},{24,20},{28,24},{5,1},{9,5},{13... | collective-permute-start | bytes 24584 | tf_op jit(solution)/shard_map/ppermute | solution.py:19
  150.2 3.4 %collective-permute-start.18 = (bf16[4,1,8,128]{3,2,0,1:T(8,128)(2,1)S(1)}, bf16[4,1,8,128]{3,2,0,1:T(8,128)(2,1)S(1)}, u32[]{:S(2)}, u32[]{:S(2)}) collective-permute-start(bf16[4,1,8,128]{3,2,0,1:T(8,128)(2,1)S(1)} %pad_maximum_fusion.4), channel_id=1, source_target_pairs={{0,4},{4,8},{8,12},{12,16},{16,20},{20,24},{24,28},{1,5},{5,9},{9,... | collective-permute-start | bytes 24584 | tf_op jit(solution)/shard_map/ppermute | solution.py:17
  153.6 0.6 copy.50
  154.2 2.6 %collective-permute-done.18 = bf16[4,1,8,128]{3,2,0,1:T(8,128)(2,1)S(1)} collective-permute-done((bf16[4,1,8,128]{3,2,0,1:T(8,128)(2,1)S(1)}, bf16[4,1,8,128]{3,2,0,1:T(8,128)(2,1)S(1)}, u32[]{:S(2)}, u32[]{:S(2)}) %collective-permute-start.18) | collective-permute-done | bytes 8224 | tf_op jit(solution)/shard_map/ppermute | solution.py:17
  158.6 1.0 fusion
  159.7 0.6 copy.51
  (93 shorter events, 10.2 us)
Async XLA Ops:
  0.6 38.6 %copy-start = (bf16[2,1,2,27,128,128]{5,4,3,2,1,0:T(8,128)(2,1)S(1)}, bf16[2,1,2,27,128,128]{5,4,3,2,1,0:T(8,128)(2,1)}, u32[]{:S(2)}) copy-start(bf16[2,1,2,27,128,128]{5,4,3,2,1,0:T(8,128)(2,1)} %param.5) | copy-start | bytes 10616836
  0.6 44.9 %copy-start.1 = (s32[2,1,8]{2,1,0:T(1,128)S(1)}, s32[2,1,8]{2,1,0:T(1,128)}, u32[]{:S(2)}) copy-start(s32[2,1,8]{2,1,0:T(1,128)} %param.7) | copy-start | bytes 196
  10.7 11.9 %collective-permute-start = (bf16[1,1,8,128]{3,2,0,1:T(8,128)(2,1)}, bf16[1,1,8,128]{3,2,0,1:T(8,128)(2,1)S(1)}, u32[]{:S(2)}, u32[]{:S(2)}) collective-permute-start(bf16[1,1,8,128]{3,2,0,1:T(8,128)(2,1)} %get-tuple-element.24), channel_id=1, source_target_pairs={{0,32},{32,64},{64,96},{96,128},{128,160},{160,192},{192,224},{1,3... | collective-permute-start | bytes 6152 | tf_op jit(solution)/shard_map/ppermute | solution.py:17
  18.5 7.2 %collective-permute-start.1 = (bf16[1,1,8,128]{3,2,1,0:T(8,128)(2,1)}, bf16[1,1,8,128]{3,2,1,0:T(8,128)(2,1)S(1)}, u32[]{:S(2)}, u32[]{:S(2)}) collective-permute-start(bf16[1,1,8,128]{3,2,1,0:T(8,128)(2,1)} %get-tuple-element.25), channel_id=1, source_target_pairs={{32,0},{64,32},{96,64},{128,96},{160,128},{192,160},{224,192},{33,... | collective-permute-start | bytes 6152 | tf_op jit(solution)/shard_map/ppermute | solution.py:19
  21.0 19.2 %copy-start.3 = (f32[2,1,2,128]{3,2,1,0:T(2,128)S(1)}, f32[2,1,2,128]{3,2,1,0:T(2,128)}, u32[]{:S(2)}) copy-start(f32[2,1,2,128]{3,2,1,0:T(2,128)} %param.9) | copy-start | bytes 6148
  25.7 7.1 %collective-permute-start.3 = (bf16[4,1,8,128]{3,2,0,1:T(8,128)(2,1)S(1)}, bf16[4,1,8,128]{3,2,0,1:T(8,128)(2,1)S(1)}, u32[]{:S(2)}, u32[]{:S(2)}) collective-permute-start(bf16[4,1,8,128]{3,2,0,1:T(8,128)(2,1)S(1)} %pad_maximum_fusion), channel_id=1, source_target_pairs={{4,0},{8,4},{12,8},{16,12},{20,16},{24,20},{28,24},{5,1},{9,5},{13... | collective-permute-start | bytes 24584 | tf_op jit(solution)/shard_map/ppermute | solution.py:19
  30.8 6.5 %collective-permute-start.2 = (bf16[4,1,8,128]{3,2,0,1:T(8,128)(2,1)S(1)}, bf16[4,1,8,128]{3,2,0,1:T(8,128)(2,1)S(1)}, u32[]{:S(2)}, u32[]{:S(2)}) collective-permute-start(bf16[4,1,8,128]{3,2,0,1:T(8,128)(2,1)S(1)} %pad_maximum_fusion), channel_id=1, source_target_pairs={{0,4},{4,8},{8,12},{12,16},{16,20},{20,24},{24,28},{1,5},{5,9},{9,... | collective-permute-start | bytes 24584 | tf_op jit(solution)/shard_map/ppermute | solution.py:17
  45.7 7.7 %collective-permute-start.4 = (bf16[1,1,8,128]{3,2,0,1:T(8,128)(2,1)S(1)}, bf16[1,1,8,128]{3,2,0,1:T(8,128)(2,1)S(1)}, u32[]{:S(2)}, u32[]{:S(2)}) collective-permute-start(bf16[1,1,8,128]{3,2,0,1:T(8,128)(2,1)S(1)} %get-tuple-element.22), channel_id=1, source_target_pairs={{0,32},{32,64},{64,96},{96,128},{128,160},{160,192},{192,224},{1,3... | collective-permute-start | bytes 6152 | tf_op jit(solution)/shard_map/ppermute | solution.py:17
  51.4 7.0 %collective-permute-start.5 = (bf16[1,1,8,128]{3,2,1,0:T(8,128)(2,1)S(1)}, bf16[1,1,8,128]{3,2,1,0:T(8,128)(2,1)S(1)}, u32[]{:S(2)}, u32[]{:S(2)}) collective-permute-start(bf16[1,1,8,128]{3,2,1,0:T(8,128)(2,1)S(1)} %get-tuple-element.23), channel_id=1, source_target_pairs={{32,0},{64,32},{96,64},{128,96},{160,128},{192,160},{224,192},{33,... | collective-permute-start | bytes 6152 | tf_op jit(solution)/shard_map/ppermute | solution.py:19
  58.5 5.3 %collective-permute-start.7 = (bf16[4,1,8,128]{3,2,0,1:T(8,128)(2,1)S(1)}, bf16[4,1,8,128]{3,2,0,1:T(8,128)(2,1)S(1)}, u32[]{:S(2)}, u32[]{:S(2)}) collective-permute-start(bf16[4,1,8,128]{3,2,0,1:T(8,128)(2,1)S(1)} %pad_maximum_fusion.1), channel_id=1, source_target_pairs={{4,0},{8,4},{12,8},{16,12},{20,16},{24,20},{28,24},{5,1},{9,5},{13... | collective-permute-start | bytes 24584 | tf_op jit(solution)/shard_map/ppermute | solution.py:19
  60.4 6.5 %collective-permute-start.6 = (bf16[4,1,8,128]{3,2,0,1:T(8,128)(2,1)S(1)}, bf16[4,1,8,128]{3,2,0,1:T(8,128)(2,1)S(1)}, u32[]{:S(2)}, u32[]{:S(2)}) collective-permute-start(bf16[4,1,8,128]{3,2,0,1:T(8,128)(2,1)S(1)} %pad_maximum_fusion.1), channel_id=1, source_target_pairs={{0,4},{4,8},{8,12},{12,16},{16,20},{20,24},{24,28},{1,5},{5,9},{9,... | collective-permute-start | bytes 24584 | tf_op jit(solution)/shard_map/ppermute | solution.py:17
  76.9 7.0 %collective-permute-start.8 = (bf16[1,1,8,128]{3,2,0,1:T(8,128)(2,1)S(1)}, bf16[1,1,8,128]{3,2,0,1:T(8,128)(2,1)S(1)}, u32[]{:S(2)}, u32[]{:S(2)}) collective-permute-start(bf16[1,1,8,128]{3,2,0,1:T(8,128)(2,1)S(1)} %get-tuple-element.20), channel_id=1, source_target_pairs={{0,32},{32,64},{64,96},{96,128},{128,160},{160,192},{192,224},{1,3... | collective-permute-start | bytes 6152 | tf_op jit(solution)/shard_map/ppermute | solution.py:17
  82.1 7.0 %collective-permute-start.9 = (bf16[1,1,8,128]{3,2,1,0:T(8,128)(2,1)S(1)}, bf16[1,1,8,128]{3,2,1,0:T(8,128)(2,1)S(1)}, u32[]{:S(2)}, u32[]{:S(2)}) collective-permute-start(bf16[1,1,8,128]{3,2,1,0:T(8,128)(2,1)S(1)} %get-tuple-element.21), channel_id=1, source_target_pairs={{32,0},{64,32},{96,64},{128,96},{160,128},{192,160},{224,192},{33,... | collective-permute-start | bytes 6152 | tf_op jit(solution)/shard_map/ppermute | solution.py:19
  89.1 5.3 %collective-permute-start.11 = (bf16[4,1,8,128]{3,2,0,1:T(8,128)(2,1)S(1)}, bf16[4,1,8,128]{3,2,0,1:T(8,128)(2,1)S(1)}, u32[]{:S(2)}, u32[]{:S(2)}) collective-permute-start(bf16[4,1,8,128]{3,2,0,1:T(8,128)(2,1)S(1)} %pad_maximum_fusion.2), channel_id=1, source_target_pairs={{4,0},{8,4},{12,8},{16,12},{20,16},{24,20},{28,24},{5,1},{9,5},{13... | collective-permute-start | bytes 24584 | tf_op jit(solution)/shard_map/ppermute | solution.py:19
  91.0 6.5 %collective-permute-start.10 = (bf16[4,1,8,128]{3,2,0,1:T(8,128)(2,1)S(1)}, bf16[4,1,8,128]{3,2,0,1:T(8,128)(2,1)S(1)}, u32[]{:S(2)}, u32[]{:S(2)}) collective-permute-start(bf16[4,1,8,128]{3,2,0,1:T(8,128)(2,1)S(1)} %pad_maximum_fusion.2), channel_id=1, source_target_pairs={{0,4},{4,8},{8,12},{12,16},{16,20},{20,24},{24,28},{1,5},{5,9},{9,... | collective-permute-start | bytes 24584 | tf_op jit(solution)/shard_map/ppermute | solution.py:17
  100.4 28.6 %copy-start.2 = (f32[2,1,2,128]{3,2,1,0:T(2,128)S(1)}, f32[2,1,2,128]{3,2,1,0:T(2,128)}, u32[]{:S(2)}) copy-start(f32[2,1,2,128]{3,2,1,0:T(2,128)} %param.8) | copy-start | bytes 6148
  105.8 6.8 %collective-permute-start.12 = (bf16[1,1,8,128]{3,2,0,1:T(8,128)(2,1)S(1)}, bf16[1,1,8,128]{3,2,0,1:T(8,128)(2,1)S(1)}, u32[]{:S(2)}, u32[]{:S(2)}) collective-permute-start(bf16[1,1,8,128]{3,2,0,1:T(8,128)(2,1)S(1)} %get-tuple-element.18), channel_id=1, source_target_pairs={{0,32},{32,64},{64,96},{96,128},{128,160},{160,192},{192,224},{1,3... | collective-permute-start | bytes 6152 | tf_op jit(solution)/shard_map/ppermute | solution.py:17
  110.7 7.0 %collective-permute-start.13 = (bf16[1,1,8,128]{3,2,1,0:T(8,128)(2,1)S(1)}, bf16[1,1,8,128]{3,2,1,0:T(8,128)(2,1)S(1)}, u32[]{:S(2)}, u32[]{:S(2)}) collective-permute-start(bf16[1,1,8,128]{3,2,1,0:T(8,128)(2,1)S(1)} %get-tuple-element.19), channel_id=1, source_target_pairs={{32,0},{64,32},{96,64},{128,96},{160,128},{192,160},{224,192},{33,... | collective-permute-start | bytes 6152 | tf_op jit(solution)/shard_map/ppermute | solution.py:19
  117.7 5.3 %collective-permute-start.15 = (bf16[4,1,8,128]{3,2,0,1:T(8,128)(2,1)S(1)}, bf16[4,1,8,128]{3,2,0,1:T(8,128)(2,1)S(1)}, u32[]{:S(2)}, u32[]{:S(2)}) collective-permute-start(bf16[4,1,8,128]{3,2,0,1:T(8,128)(2,1)S(1)} %pad_maximum_fusion.3), channel_id=1, source_target_pairs={{4,0},{8,4},{12,8},{16,12},{20,16},{24,20},{28,24},{5,1},{9,5},{13... | collective-permute-start | bytes 24584 | tf_op jit(solution)/shard_map/ppermute | solution.py:19
  119.6 6.5 %collective-permute-start.14 = (bf16[4,1,8,128]{3,2,0,1:T(8,128)(2,1)S(1)}, bf16[4,1,8,128]{3,2,0,1:T(8,128)(2,1)S(1)}, u32[]{:S(2)}, u32[]{:S(2)}) collective-permute-start(bf16[4,1,8,128]{3,2,0,1:T(8,128)(2,1)S(1)} %pad_maximum_fusion.3), channel_id=1, source_target_pairs={{0,4},{4,8},{8,12},{12,16},{16,20},{20,24},{24,28},{1,5},{5,9},{9,... | collective-permute-start | bytes 24584 | tf_op jit(solution)/shard_map/ppermute | solution.py:17
  136.2 7.0 %collective-permute-start.16 = (bf16[1,1,8,128]{3,2,0,1:T(8,128)(2,1)S(1)}, bf16[1,1,8,128]{3,2,0,1:T(8,128)(2,1)S(1)}, u32[]{:S(2)}, u32[]{:S(2)}) collective-permute-start(bf16[1,1,8,128]{3,2,0,1:T(8,128)(2,1)S(1)} %get-tuple-element.16), channel_id=1, source_target_pairs={{0,32},{32,64},{64,96},{96,128},{128,160},{160,192},{192,224},{1,3... | collective-permute-start | bytes 6152 | tf_op jit(solution)/shard_map/ppermute | solution.py:17
  141.3 7.0 %collective-permute-start.17 = (bf16[1,1,8,128]{3,2,1,0:T(8,128)(2,1)S(1)}, bf16[1,1,8,128]{3,2,1,0:T(8,128)(2,1)S(1)}, u32[]{:S(2)}, u32[]{:S(2)}) collective-permute-start(bf16[1,1,8,128]{3,2,1,0:T(8,128)(2,1)S(1)} %get-tuple-element.17), channel_id=1, source_target_pairs={{32,0},{64,32},{96,64},{128,96},{160,128},{192,160},{224,192},{33,... | collective-permute-start | bytes 6152 | tf_op jit(solution)/shard_map/ppermute | solution.py:19
  148.3 5.9 %collective-permute-start.19 = (bf16[4,1,8,128]{3,2,0,1:T(8,128)(2,1)S(1)}, bf16[4,1,8,128]{3,2,0,1:T(8,128)(2,1)S(1)}, u32[]{:S(2)}, u32[]{:S(2)}) collective-permute-start(bf16[4,1,8,128]{3,2,0,1:T(8,128)(2,1)S(1)} %pad_maximum_fusion.4), channel_id=1, source_target_pairs={{4,0},{8,4},{12,8},{16,12},{20,16},{24,20},{28,24},{5,1},{9,5},{13... | collective-permute-start | bytes 24584 | tf_op jit(solution)/shard_map/ppermute | solution.py:19
  150.2 6.5 %collective-permute-start.18 = (bf16[4,1,8,128]{3,2,0,1:T(8,128)(2,1)S(1)}, bf16[4,1,8,128]{3,2,0,1:T(8,128)(2,1)S(1)}, u32[]{:S(2)}, u32[]{:S(2)}) collective-permute-start(bf16[4,1,8,128]{3,2,0,1:T(8,128)(2,1)S(1)} %pad_maximum_fusion.4), channel_id=1, source_target_pairs={{0,4},{4,8},{8,12},{12,16},{16,20},{20,24},{24,28},{1,5},{5,9},{9,... | collective-permute-start | bytes 24584 | tf_op jit(solution)/shard_map/ppermute | solution.py:17
where the time goes:
time: 161 us; the launch traced here: 160 us
  starting transfers between devices  66.3 us (41%)
  waiting for transfers between devices  39.9 us (25%)
  blocking collectives  32.3 us (20%)
  matrix products  15.5 us (10%)
  local copies, waits for them, and re-layouts  3.64 us (2%)
  other arithmetic  1.62 us (1%)
    ppermute x10, starting transfers between devices, padded_2(): lax.ppermute(tail, axis, [(i, (i + 1) % count) for i in range(ends)])  44 us
    all_gather x5, blocking collectives, operator(): lax.all_gather(vector.astype(jnp.bfloat16), 'gz', axis=2, tiled=True)  32.3 us
    ppermute x10, waiting for transfers between devices, padded_2(): lax.ppermute(head, axis, [((i + 1) % count, i) for i in range(ends)])  23.5 us
    ppermute x10, starting transfers between devices, padded_2(): lax.ppermute(head, axis, [((i + 1) % count, i) for i in range(ends)])  22.3 us
    ppermute x10, waiting for transfers between devices, padded_2(): lax.ppermute(tail, axis, [(i, (i + 1) % count) for i in range(ends)])  16.4 us
    dot_general x45, matrix products, coupled_product(): jnp.einsum('xyscp,xypw->xyscw', table, column, preferred_element_type=jnp...  9.05 us
    dot_general x5, matrix products, coupled_product(): jnp.einsum('xysoj,xysoij->xysi', gathered, matrix, preferred_element_type...  5.22 us
  transfers between devices with their start and end apart: 20, of which 10 were waited for; matrix products, arithmetic and copies ran while one was open for 2% of the time, Pallas kernels for 0%

commit v1 on v0

--- a/solution.py
+++ b/solution.py
@@ -4,6 +4,28 @@
 from jax.sharding import PartitionSpec as P
 
 DEG = 4
+
+
+def quotas_match(x_local):
+    named_axis = "gz"
+    passed, carry, after = (
+        jax.lax.axis_size(named_axis),
+        jax.lax.axis_index(named_axis),
+        x_local.shape[2],
+    )
+    steps_seen = list(map(lambda src_i: (src_i, (src_i + 1) % passed), range(passed)))
+    queue = list(map(lambda src_i: (src_i, (src_i - 1) % passed), range(passed)))
+    w1 = jnp.zeros((*x_local.shape[:2], passed * after, *x_local.shape[3:]), x_local.dtype)
+    w1 = lax.dynamic_update_slice_in_dim(w1, x_local, carry * after, axis=2)
+    seen_now = wide_out = x_local
+    kept_arr = passed // 2
+    for b in range(1, kept_arr + 1):
+        seen_now = jax.lax.ppermute(seen_now, axis_name=named_axis, perm=steps_seen)
+        w1 = lax.dynamic_update_slice_in_dim(w1, seen_now, (carry - b) % passed * after, axis=2)
+        if b < passed - kept_arr:
+            wide_out = jax.lax.ppermute(wide_out, perm=queue, axis_name=named_axis)
+            w1 = lax.dynamic_update_slice_in_dim(w1, wide_out, (carry + b) % passed * after, axis=2)
+    return w1
 
 
 def padded_2(cells, sides, width):
@@ -63,7 +85,7 @@
     present = lax.dynamic_slice_in_dim(pattern, first, depth, 2)
 
     def operator(vector):
-        column = lax.all_gather(vector.astype(jnp.bfloat16), "gz", axis=2, tiled=True)
+        column = quotas_match(vector.astype(jnp.bfloat16))
         planes = by_plane(column, order)
         return coupled_product(blocks, planes, rows, present)
 

time: 161 us -> 167 us (1.037); the launches traced: 160 us -> 164 us
  starting transfers between devices: 66.3 us -> 108 us
  blocking collectives: 32.3 us -> 0 us
  waiting for transfers between devices: 39.9 us -> 27.2 us
  matrix products: 15.5 us -> 20.9 us
    all_gather x5 -> x0, blocking collectives: 32.3 us -> none  [operator(): lax.all_gather(vector.astype(jnp.bfloat16), 'gz', axis=2, tiled=True)]
    ppermute x10, starting transfers between devices: 22.3 us -> 45.5 us  [padded_2(): lax.ppermute(head, axis, [((i + 1) % count, i) for i in range(ends)])]
    ppermute x0 -> x15, waiting for transfers between devices: none -> 20.6 us  [the longest x10 20.6 us: quotas_match(): seen_now = jax.lax.ppermute(seen_now, axis_name=named_axis, perm=steps_seen)]
    ppermute x10, waiting for transfers between devices: 23.5 us -> 3.75 us  [padded_2(): lax.ppermute(head, axis, [((i + 1) % count, i) for i in range(ends)])]
    ppermute x0 -> x15, starting transfers between devices: none -> 13.8 us  [the longest x5 12.1 us: quotas_match(): wide_out = jax.lax.ppermute(wide_out, perm=queue, axis_name=named_axis)]
    ppermute x10, waiting for transfers between devices: 16.4 us -> 2.83 us  [padded_2(): lax.ppermute(tail, axis, [(i, (i + 1) % count) for i in range(ends)])]
    dot_general x45, matrix products: 9.05 us -> 14.4 us  [coupled_product(): jnp.einsum('xyscp,xypw->xyscw', table, column, preferred_element_type=jnp...]
    ppermute x10, starting transfers between devices: 44 us -> 49.2 us  [padded_2(): lax.ppermute(tail, axis, [(i, (i + 1) % count) for i in range(ends)])]
  transfers between devices with their start and end apart: 20 -> 35, of which waited for: 10 -> 18; matrix products, arithmetic and copies ran while one was open for 2% -> 2% of each run, Pallas kernels for 0% -> 0%
where the time goes in v1:
time: 167 us; the launch traced here: 164 us
  starting transfers between devices  108 us (65%)
  waiting for transfers between devices  27.2 us (16%)
  matrix products  20.9 us (13%)
  local copies, waits for them, and re-layouts  3.18 us (2%)
  other arithmetic  3.08 us (2%)
    ppermute x10, starting transfers between devices, padded_2(): lax.ppermute(tail, axis, [(i, (i + 1) % count) for i in range(ends)])  49.2 us
    ppermute x10, starting transfers between devices, padded_2(): lax.ppermute(head, axis, [((i + 1) % count, i) for i in range(ends)])  45.5 us
    ppermute x10, waiting for transfers between devices, quotas_match(): seen_now = jax.lax.ppermute(seen_now, axis_name=named_axis, perm=steps_seen)  20.6 us
    dot_general x45, matrix products, coupled_product(): jnp.einsum('xyscp,xypw->xyscw', table, column, preferred_element_type=jnp...  14.4 us
    ppermute x5, starting transfers between devices, quotas_match(): wide_out = jax.lax.ppermute(wide_out, perm=queue, axis_name=named_axis)  12.1 us
    dot_general x5, matrix products, coupled_product(): jnp.einsum('xysoj,xysoij->xysi', gathered, matrix, preferred_element_type...  5.22 us
    ppermute x10, waiting for transfers between devices, padded_2(): lax.ppermute(head, axis, [((i + 1) % count, i) for i in range(ends)])  3.75 us
  transfers between devices with their start and end apart: 35, of which 18 were waited for; matrix products, arithmetic and copies ran while one was open for 2% of the time, Pallas kernels for 0%

profile of v1, /device:TPU:97, one launch (start us, length us, event | category | flops | bytes accessed | tf_op | source)
XLA Modules:
  0.0 163.9 jit_solution(2815850605844230179)
XLA Ops:
  0.7 1.4 constant_dynamic-update-slice_fusion.19
  2.1 1.2 collective-permute-start
  3.3 1.5 collective-permute-start.1
  7.6 2.3 %collective-permute-done.2 = bf16[2,1,2,128]{3,2,1,0:T(2,128)(2,1)S(1)} collective-permute-done((bf16[2,1,2,128]{3,2,1,0:T(2,128)(2,1)}, bf16[2,1,2,128]{3,2,1,0:T(2,128)(2,1)S(1)}, u32[]{:S(2)}, u32[]{:S(2)}) %collective-permute-start.2) | collective-permute-done | bytes 1056 | tf_op jit(solution)/shard_map/ppermute | solution.py:23
  10.8 4.8 %collective-permute-start.4 = (bf16[1,1,8,128]{3,2,1,0:T(8,128)(2,1)S(1)}, bf16[1,1,8,128]{3,2,1,0:T(8,128)(2,1)S(1)}, u32[]{:S(2)}, u32[]{:S(2)}) collective-permute-start(bf16[1,1,8,128]{3,2,1,0:T(8,128)(2,1)S(1)} %get-tuple-element.26), channel_id=1, source_target_pairs={{32,0},{64,32},{96,64},{128,96},{160,128},{192,160},{224,192},{33,... | collective-permute-start | bytes 6152 | tf_op jit(solution)/shard_map/ppermute | solution.py:41
  15.6 5.1 %collective-permute-start.3 = (bf16[1,1,8,128]{3,2,0,1:T(8,128)(2,1)S(1)}, bf16[1,1,8,128]{3,2,0,1:T(8,128)(2,1)S(1)}, u32[]{:S(2)}, u32[]{:S(2)}) collective-permute-start(bf16[1,1,8,128]{3,2,0,1:T(8,128)(2,1)S(1)} %get-tuple-element.25), channel_id=1, source_target_pairs={{0,32},{32,64},{64,96},{96,128},{128,160},{160,192},{192,224},{1,3... | collective-permute-start | bytes 6152 | tf_op jit(solution)/shard_map/ppermute | solution.py:39
  21.5 3.2 %collective-permute-start.5 = (bf16[4,1,8,128]{3,2,0,1:T(8,128)(2,1)S(1)}, bf16[4,1,8,128]{3,2,0,1:T(8,128)(2,1)S(1)}, u32[]{:S(2)}, u32[]{:S(2)}) collective-permute-start(bf16[4,1,8,128]{3,2,0,1:T(8,128)(2,1)S(1)} %pad_maximum_fusion), channel_id=1, source_target_pairs={{0,4},{4,8},{8,12},{12,16},{16,20},{20,24},{24,28},{1,5},{5,9},{9,... | collective-permute-start | bytes 24584 | tf_op jit(solution)/shard_map/ppermute | solution.py:39
  24.7 4.2 %collective-permute-start.6 = (bf16[4,1,8,128]{3,2,0,1:T(8,128)(2,1)S(1)}, bf16[4,1,8,128]{3,2,0,1:T(8,128)(2,1)S(1)}, u32[]{:S(2)}, u32[]{:S(2)}) collective-permute-start(bf16[4,1,8,128]{3,2,0,1:T(8,128)(2,1)S(1)} %pad_maximum_fusion), channel_id=1, source_target_pairs={{4,0},{8,4},{12,8},{16,12},{20,16},{24,20},{28,24},{5,1},{9,5},{13... | collective-permute-start | bytes 24584 | tf_op jit(solution)/shard_map/ppermute | solution.py:41
  30.5 0.9 fusion.13
  31.4 0.9 fusion.15
  32.3 0.9 fusion.17
  33.2 0.9 fusion.19
  34.1 0.9 fusion.21
  34.9 0.9 fusion.23
  35.8 0.9 fusion.25
  36.9 1.0 fusion.8
  38.1 2.7 %collective-permute-start.8 = (bf16[2,1,2,128]{3,2,1,0:T(2,128)(2,1)S(1)}, bf16[2,1,2,128]{3,2,1,0:T(2,128)(2,1)S(1)}, u32[]{:S(2)}, u32[]{:S(2)}) collective-permute-start(bf16[2,1,2,128]{3,2,1,0:T(2,128)(2,1)S(1)} %get-tuple-element.13), channel_id=1, source_target_pairs={{0,3},{1,0},{2,1},{3,2},{4,7},{5,4},{6,5},{7,6},{8,11},{9,8},{10,9... | collective-permute-start | bytes 3080 | tf_op jit(solution)/shard_map/ppermute | solution.py:26
  40.8 1.0 collective-permute-done.7
  41.7 3.6 %collective-permute-done.9 = bf16[2,1,2,128]{3,2,1,0:T(2,128)(2,1)S(1)} collective-permute-done((bf16[2,1,2,128]{3,2,1,0:T(2,128)(2,1)S(1)}, bf16[2,1,2,128]{3,2,1,0:T(2,128)(2,1)S(1)}, u32[]{:S(2)}, u32[]{:S(2)}) %collective-permute-start.9) | collective-permute-done | bytes 1056 | tf_op jit(solution)/shard_map/ppermute | solution.py:23
  45.5 5.2 %collective-permute-start.11 = (bf16[1,1,8,128]{3,2,1,0:T(8,128)(2,1)S(1)}, bf16[1,1,8,128]{3,2,1,0:T(8,128)(2,1)S(1)}, u32[]{:S(2)}, u32[]{:S(2)}) collective-permute-start(bf16[1,1,8,128]{3,2,1,0:T(8,128)(2,1)S(1)} %get-tuple-element.24), channel_id=1, source_target_pairs={{32,0},{64,32},{96,64},{128,96},{160,128},{192,160},{224,192},{33,... | collective-permute-start | bytes 6152 | tf_op jit(solution)/shard_map/ppermute | solution.py:41
  50.7 6.3 %collective-permute-start.10 = (bf16[1,1,8,128]{3,2,0,1:T(8,128)(2,1)S(1)}, bf16[1,1,8,128]{3,2,0,1:T(8,128)(2,1)S(1)}, u32[]{:S(2)}, u32[]{:S(2)}) collective-permute-start(bf16[1,1,8,128]{3,2,0,1:T(8,128)(2,1)S(1)} %get-tuple-element.23), channel_id=1, source_target_pairs={{0,32},{32,64},{64,96},{96,128},{128,160},{160,192},{192,224},{1,3... | collective-permute-start | bytes 6152 | tf_op jit(solution)/shard_map/ppermute | solution.py:39
  57.8 2.9 %collective-permute-start.12 = (bf16[4,1,8,128]{3,2,0,1:T(8,128)(2,1)S(1)}, bf16[4,1,8,128]{3,2,0,1:T(8,128)(2,1)S(1)}, u32[]{:S(2)}, u32[]{:S(2)}) collective-permute-start(bf16[4,1,8,128]{3,2,0,1:T(8,128)(2,1)S(1)} %pad_maximum_fusion.1), channel_id=1, source_target_pairs={{0,4},{4,8},{8,12},{12,16},{16,20},{20,24},{24,28},{1,5},{5,9},{9,... | collective-permute-start | bytes 24584 | tf_op jit(solution)/shard_map/ppermute | solution.py:39
  60.7 5.0 %collective-permute-start.13 = (bf16[4,1,8,128]{3,2,0,1:T(8,128)(2,1)S(1)}, bf16[4,1,8,128]{3,2,0,1:T(8,128)(2,1)S(1)}, u32[]{:S(2)}, u32[]{:S(2)}) collective-permute-start(bf16[4,1,8,128]{3,2,0,1:T(8,128)(2,1)S(1)} %pad_maximum_fusion.1), channel_id=1, source_target_pairs={{4,0},{8,4},{12,8},{16,12},{20,16},{24,20},{28,24},{5,1},{9,5},{13... | collective-permute-start | bytes 24584 | tf_op jit(solution)/shard_map/ppermute | solution.py:41
  68.4 1.0 fusion.6
  69.6 2.7 %collective-permute-start.15 = (bf16[2,1,2,128]{3,2,1,0:T(2,128)(2,1)S(1)}, bf16[2,1,2,128]{3,2,1,0:T(2,128)(2,1)S(1)}, u32[]{:S(2)}, u32[]{:S(2)}) collective-permute-start(bf16[2,1,2,128]{3,2,1,0:T(2,128)(2,1)S(1)} %get-tuple-element.10), channel_id=1, source_target_pairs={{0,3},{1,0},{2,1},{3,2},{4,7},{5,4},{6,5},{7,6},{8,11},{9,8},{10,9... | collective-permute-start | bytes 3080 | tf_op jit(solution)/shard_map/ppermute | solution.py:26
  72.3 1.0 collective-permute-done.14
  73.3 3.6 %collective-permute-done.16 = bf16[2,1,2,128]{3,2,1,0:T(2,128)(2,1)S(1)} collective-permute-done((bf16[2,1,2,128]{3,2,1,0:T(2,128)(2,1)S(1)}, bf16[2,1,2,128]{3,2,1,0:T(2,128)(2,1)S(1)}, u32[]{:S(2)}, u32[]{:S(2)}) %collective-permute-start.16) | collective-permute-done | bytes 1056 | tf_op jit(solution)/shard_map/ppermute | solution.py:23
  77.0 3.8 %collective-permute-start.18 = (bf16[1,1,8,128]{3,2,1,0:T(8,128)(2,1)S(1)}, bf16[1,1,8,128]{3,2,1,0:T(8,128)(2,1)S(1)}, u32[]{:S(2)}, u32[]{:S(2)}) collective-permute-start(bf16[1,1,8,128]{3,2,1,0:T(8,128)(2,1)S(1)} %get-tuple-element.22), channel_id=1, source_target_pairs={{32,0},{64,32},{96,64},{128,96},{160,128},{192,160},{224,192},{33,... | collective-permute-start | bytes 6152 | tf_op jit(solution)/shard_map/ppermute | solution.py:41
  80.8 7.5 %collective-permute-start.17 = (bf16[1,1,8,128]{3,2,0,1:T(8,128)(2,1)S(1)}, bf16[1,1,8,128]{3,2,0,1:T(8,128)(2,1)S(1)}, u32[]{:S(2)}, u32[]{:S(2)}) collective-permute-start(bf16[1,1,8,128]{3,2,0,1:T(8,128)(2,1)S(1)} %get-tuple-element.21), channel_id=1, source_target_pairs={{0,32},{32,64},{64,96},{96,128},{128,160},{160,192},{192,224},{1,3... | collective-permute-start | bytes 6152 | tf_op jit(solution)/shard_map/ppermute | solution.py:39
  89.1 2.1 %collective-permute-start.19 = (bf16[4,1,8,128]{3,2,0,1:T(8,128)(2,1)S(1)}, bf16[4,1,8,128]{3,2,0,1:T(8,128)(2,1)S(1)}, u32[]{:S(2)}, u32[]{:S(2)}) collective-permute-start(bf16[4,1,8,128]{3,2,0,1:T(8,128)(2,1)S(1)} %pad_maximum_fusion.2), channel_id=1, source_target_pairs={{0,4},{4,8},{8,12},{12,16},{16,20},{20,24},{24,28},{1,5},{5,9},{9,... | collective-permute-start | bytes 24584 | tf_op jit(solution)/shard_map/ppermute | solution.py:39
  91.2 5.9 %collective-permute-start.20 = (bf16[4,1,8,128]{3,2,0,1:T(8,128)(2,1)S(1)}, bf16[4,1,8,128]{3,2,0,1:T(8,128)(2,1)S(1)}, u32[]{:S(2)}, u32[]{:S(2)}) collective-permute-start(bf16[4,1,8,128]{3,2,0,1:T(8,128)(2,1)S(1)} %pad_maximum_fusion.2), channel_id=1, source_target_pairs={{4,0},{8,4},{12,8},{16,12},{20,16},{24,20},{28,24},{5,1},{9,5},{13... | collective-permute-start | bytes 24584 | tf_op jit(solution)/shard_map/ppermute | solution.py:41
  99.7 1.0 fusion.4
  100.9 2.7 %collective-permute-start.22 = (bf16[2,1,2,128]{3,2,1,0:T(2,128)(2,1)S(1)}, bf16[2,1,2,128]{3,2,1,0:T(2,128)(2,1)S(1)}, u32[]{:S(2)}, u32[]{:S(2)}) collective-permute-start(bf16[2,1,2,128]{3,2,1,0:T(2,128)(2,1)S(1)} %get-tuple-element.6), channel_id=1, source_target_pairs={{0,3},{1,0},{2,1},{3,2},{4,7},{5,4},{6,5},{7,6},{8,11},{9,8},{10,9... | collective-permute-start | bytes 3080 | tf_op jit(solution)/shard_map/ppermute | solution.py:26
  103.5 1.0 collective-permute-done.21
  104.5 3.6 %collective-permute-done.23 = bf16[2,1,2,128]{3,2,1,0:T(2,128)(2,1)S(1)} collective-permute-done((bf16[2,1,2,128]{3,2,1,0:T(2,128)(2,1)S(1)}, bf16[2,1,2,128]{3,2,1,0:T(2,128)(2,1)S(1)}, u32[]{:S(2)}, u32[]{:S(2)}) %collective-permute-start.23) | collective-permute-done | bytes 1056 | tf_op jit(solution)/shard_map/ppermute | solution.py:23
  108.3 2.6 %collective-permute-start.25 = (bf16[1,1,8,128]{3,2,1,0:T(8,128)(2,1)S(1)}, bf16[1,1,8,128]{3,2,1,0:T(8,128)(2,1)S(1)}, u32[]{:S(2)}, u32[]{:S(2)}) collective-permute-start(bf16[1,1,8,128]{3,2,1,0:T(8,128)(2,1)S(1)} %get-tuple-element.20), channel_id=1, source_target_pairs={{32,0},{64,32},{96,64},{128,96},{160,128},{192,160},{224,192},{33,... | collective-permute-start | bytes 6152 | tf_op jit(solution)/shard_map/ppermute | solution.py:41
  110.9 8.7 %collective-permute-start.24 = (bf16[1,1,8,128]{3,2,0,1:T(8,128)(2,1)S(1)}, bf16[1,1,8,128]{3,2,0,1:T(8,128)(2,1)S(1)}, u32[]{:S(2)}, u32[]{:S(2)}) collective-permute-start(bf16[1,1,8,128]{3,2,0,1:T(8,128)(2,1)S(1)} %get-tuple-element.19), channel_id=1, source_target_pairs={{0,32},{32,64},{64,96},{96,128},{128,160},{160,192},{192,224},{1,3... | collective-permute-start | bytes 6152 | tf_op jit(solution)/shard_map/ppermute | solution.py:39
  120.4 1.9 %collective-permute-start.26 = (bf16[4,1,8,128]{3,2,0,1:T(8,128)(2,1)S(1)}, bf16[4,1,8,128]{3,2,0,1:T(8,128)(2,1)S(1)}, u32[]{:S(2)}, u32[]{:S(2)}) collective-permute-start(bf16[4,1,8,128]{3,2,0,1:T(8,128)(2,1)S(1)} %pad_maximum_fusion.3), channel_id=1, source_target_pairs={{0,4},{4,8},{8,12},{12,16},{16,20},{20,24},{24,28},{1,5},{5,9},{9,... | collective-permute-start | bytes 24584 | tf_op jit(solution)/shard_map/ppermute | solution.py:39
  122.3 6.0 %collective-permute-start.27 = (bf16[4,1,8,128]{3,2,0,1:T(8,128)(2,1)S(1)}, bf16[4,1,8,128]{3,2,0,1:T(8,128)(2,1)S(1)}, u32[]{:S(2)}, u32[]{:S(2)}) collective-permute-start(bf16[4,1,8,128]{3,2,0,1:T(8,128)(2,1)S(1)} %pad_maximum_fusion.3), channel_id=1, source_target_pairs={{4,0},{8,4},{12,8},{16,12},{20,16},{24,20},{28,24},{5,1},{9,5},{13... | collective-permute-start | bytes 24584 | tf_op jit(solution)/shard_map/ppermute | solution.py:41
  131.0 1.0 fusion.2
  132.1 2.7 %collective-permute-start.29 = (bf16[2,1,2,128]{3,2,1,0:T(2,128)(2,1)S(1)}, bf16[2,1,2,128]{3,2,1,0:T(2,128)(2,1)S(1)}, u32[]{:S(2)}, u32[]{:S(2)}) collective-permute-start(bf16[2,1,2,128]{3,2,1,0:T(2,128)(2,1)S(1)} %get-tuple-element.3), channel_id=1, source_target_pairs={{0,3},{1,0},{2,1},{3,2},{4,7},{5,4},{6,5},{7,6},{8,11},{9,8},{10,9... | collective-permute-start | bytes 3080 | tf_op jit(solution)/shard_map/ppermute | solution.py:26
  134.8 1.0 collective-permute-done.28
  135.8 3.6 %collective-permute-done.30 = bf16[2,1,2,128]{3,2,1,0:T(2,128)(2,1)S(1)} collective-permute-done((bf16[2,1,2,128]{3,2,1,0:T(2,128)(2,1)S(1)}, bf16[2,1,2,128]{3,2,1,0:T(2,128)(2,1)S(1)}, u32[]{:S(2)}, u32[]{:S(2)}) %collective-permute-start.30) | collective-permute-done | bytes 1056 | tf_op jit(solution)/shard_map/ppermute | solution.py:23
  139.5 1.9 %collective-permute-start.32 = (bf16[1,1,8,128]{3,2,1,0:T(8,128)(2,1)S(1)}, bf16[1,1,8,128]{3,2,1,0:T(8,128)(2,1)S(1)}, u32[]{:S(2)}, u32[]{:S(2)}) collective-permute-start(bf16[1,1,8,128]{3,2,1,0:T(8,128)(2,1)S(1)} %get-tuple-element.18), channel_id=1, source_target_pairs={{32,0},{64,32},{96,64},{128,96},{160,128},{192,160},{224,192},{33,... | collective-permute-start | bytes 6152 | tf_op jit(solution)/shard_map/ppermute | solution.py:41
  141.4 9.4 %collective-permute-start.31 = (bf16[1,1,8,128]{3,2,0,1:T(8,128)(2,1)S(1)}, bf16[1,1,8,128]{3,2,0,1:T(8,128)(2,1)S(1)}, u32[]{:S(2)}, u32[]{:S(2)}) collective-permute-start(bf16[1,1,8,128]{3,2,0,1:T(8,128)(2,1)S(1)} %get-tuple-element.17), channel_id=1, source_target_pairs={{0,32},{32,64},{64,96},{96,128},{128,160},{160,192},{192,224},{1,3... | collective-permute-start | bytes 6152 | tf_op jit(solution)/shard_map/ppermute | solution.py:39
  151.6 1.9 %collective-permute-start.33 = (bf16[4,1,8,128]{3,2,0,1:T(8,128)(2,1)S(1)}, bf16[4,1,8,128]{3,2,0,1:T(8,128)(2,1)S(1)}, u32[]{:S(2)}, u32[]{:S(2)}) collective-permute-start(bf16[4,1,8,128]{3,2,0,1:T(8,128)(2,1)S(1)} %pad_maximum_fusion.4), channel_id=1, source_target_pairs={{0,4},{4,8},{8,12},{12,16},{16,20},{20,24},{24,28},{1,5},{5,9},{9,... | collective-permute-start | bytes 24584 | tf_op jit(solution)/shard_map/ppermute | solution.py:39
  153.5 6.0 %collective-permute-start.34 = (bf16[4,1,8,128]{3,2,0,1:T(8,128)(2,1)S(1)}, bf16[4,1,8,128]{3,2,0,1:T(8,128)(2,1)S(1)}, u32[]{:S(2)}, u32[]{:S(2)}) collective-permute-start(bf16[4,1,8,128]{3,2,0,1:T(8,128)(2,1)S(1)} %pad_maximum_fusion.4), channel_id=1, source_target_pairs={{4,0},{8,4},{12,8},{16,12},{20,16},{24,20},{28,24},{5,1},{9,5},{13... | collective-permute-start | bytes 24584 | tf_op jit(solution)/shard_map/ppermute | solution.py:41
  162.2 1.0 fusion
  (152 shorter events, 21.5 us)
Async XLA Ops:
  0.6 36.3 %copy-start = (bf16[2,1,2,27,128,128]{5,4,3,2,1,0:T(8,128)(2,1)S(1)}, bf16[2,1,2,27,128,128]{5,4,3,2,1,0:T(8,128)(2,1)}, u32[]{:S(2)}) copy-start(bf16[2,1,2,27,128,128]{5,4,3,2,1,0:T(8,128)(2,1)} %param.5) | copy-start | bytes 10616836
  0.6 44.7 %copy-start.1 = (s32[2,1,8]{2,1,0:T(1,128)S(1)}, s32[2,1,8]{2,1,0:T(1,128)}, u32[]{:S(2)}) copy-start(s32[2,1,8]{2,1,0:T(1,128)} %param.7) | copy-start | bytes 196
  0.7 37.3 %copy-start.3 = (f32[2,1,2,128]{3,2,1,0:T(2,128)S(1)}, f32[2,1,2,128]{3,2,1,0:T(2,128)}, u32[]{:S(2)}) copy-start(f32[2,1,2,128]{3,2,1,0:T(2,128)} %param.9) | copy-start | bytes 6148
  2.1 4.1 %collective-permute-start = (bf16[2,1,2,128]{3,2,1,0:T(2,128)(2,1)}, bf16[2,1,2,128]{3,2,1,0:T(2,128)(2,1)}, u32[]{:S(2)}, u32[]{:S(2)}) collective-permute-start(bf16[2,1,2,128]{3,2,1,0:T(2,128)(2,1)} %get-tuple-element.16), channel_id=1, source_target_pairs={{0,1},{1,2},{2,3},{3,0},{4,5},{5,6},{6,7},{7,4},{8,9},{9,10},{10,1... | collective-permute-start | bytes 3080 | tf_op jit(solution)/shard_map/ppermute | solution.py:23
  3.3 3.7 %collective-permute-start.1 = (bf16[2,1,2,128]{3,2,1,0:T(2,128)(2,1)}, bf16[2,1,2,128]{3,2,1,0:T(2,128)(2,1)}, u32[]{:S(2)}, u32[]{:S(2)}) collective-permute-start(bf16[2,1,2,128]{3,2,1,0:T(2,128)(2,1)} %get-tuple-element.16), channel_id=1, source_target_pairs={{0,3},{1,0},{2,1},{3,2},{4,7},{5,4},{6,5},{7,6},{8,11},{9,8},{10,9... | collective-permute-start | bytes 3080 | tf_op jit(solution)/shard_map/ppermute | solution.py:26
  6.2 60.4 %copy-start.11 = (bf16[2,2,3]{2,1,0:T(2,128)(2,1)S(1)}, bf16[2,2,3]{2,1,0:T(2,128)(2,1)}, u32[]{:S(2)}) copy-start(bf16[2,2,3]{2,1,0:T(2,128)(2,1)} %get-tuple-element.37) | copy-start | bytes 76
  6.2 60.6 %copy-start.10 = (bf16[2,2,3]{2,1,0:T(2,128)(2,1)S(1)}, bf16[2,2,3]{2,1,0:T(2,128)(2,1)}, u32[]{:S(2)}) copy-start(bf16[2,2,3]{2,1,0:T(2,128)(2,1)} %get-tuple-element.36) | copy-start | bytes 76
  6.2 60.8 %copy-start.9 = (bf16[2,2,3]{2,1,0:T(2,128)(2,1)S(1)}, bf16[2,2,3]{2,1,0:T(2,128)(2,1)}, u32[]{:S(2)}) copy-start(bf16[2,2,3]{2,1,0:T(2,128)(2,1)} %get-tuple-element.35) | copy-start | bytes 76
  6.2 61.0 %copy-start.8 = (bf16[2,2,3]{2,1,0:T(2,128)(2,1)S(1)}, bf16[2,2,3]{2,1,0:T(2,128)(2,1)}, u32[]{:S(2)}) copy-start(bf16[2,2,3]{2,1,0:T(2,128)(2,1)} %get-tuple-element.34) | copy-start | bytes 76
  6.2 3.8 %collective-permute-start.2 = (bf16[2,1,2,128]{3,2,1,0:T(2,128)(2,1)}, bf16[2,1,2,128]{3,2,1,0:T(2,128)(2,1)S(1)}, u32[]{:S(2)}, u32[]{:S(2)}) collective-permute-start(bf16[2,1,2,128]{3,2,1,0:T(2,128)(2,1)} %collective-permute-done), channel_id=1, source_target_pairs={{0,1},{1,2},{2,3},{3,0},{4,5},{5,6},{6,7},{7,4},{8,9},{9,10},{10,1... | collective-permute-start | bytes 3080 | tf_op jit(solution)/shard_map/ppermute | solution.py:23
  10.8 10.7 %collective-permute-start.4 = (bf16[1,1,8,128]{3,2,1,0:T(8,128)(2,1)S(1)}, bf16[1,1,8,128]{3,2,1,0:T(8,128)(2,1)S(1)}, u32[]{:S(2)}, u32[]{:S(2)}) collective-permute-start(bf16[1,1,8,128]{3,2,1,0:T(8,128)(2,1)S(1)} %get-tuple-element.26), channel_id=1, source_target_pairs={{32,0},{64,32},{96,64},{128,96},{160,128},{192,160},{224,192},{33,... | collective-permute-start | bytes 6152 | tf_op jit(solution)/shard_map/ppermute | solution.py:41
  15.6 5.9 %collective-permute-start.3 = (bf16[1,1,8,128]{3,2,0,1:T(8,128)(2,1)S(1)}, bf16[1,1,8,128]{3,2,0,1:T(8,128)(2,1)S(1)}, u32[]{:S(2)}, u32[]{:S(2)}) collective-permute-start(bf16[1,1,8,128]{3,2,0,1:T(8,128)(2,1)S(1)} %get-tuple-element.25), channel_id=1, source_target_pairs={{0,32},{32,64},{64,96},{96,128},{128,160},{160,192},{192,224},{1,3... | collective-permute-start | bytes 6152 | tf_op jit(solution)/shard_map/ppermute | solution.py:39
  21.5 7.5 %collective-permute-start.5 = (bf16[4,1,8,128]{3,2,0,1:T(8,128)(2,1)S(1)}, bf16[4,1,8,128]{3,2,0,1:T(8,128)(2,1)S(1)}, u32[]{:S(2)}, u32[]{:S(2)}) collective-permute-start(bf16[4,1,8,128]{3,2,0,1:T(8,128)(2,1)S(1)} %pad_maximum_fusion), channel_id=1, source_target_pairs={{0,4},{4,8},{8,12},{12,16},{16,20},{20,24},{24,28},{1,5},{5,9},{9,... | collective-permute-start | bytes 24584 | tf_op jit(solution)/shard_map/ppermute | solution.py:39
  24.7 5.0 %collective-permute-start.6 = (bf16[4,1,8,128]{3,2,0,1:T(8,128)(2,1)S(1)}, bf16[4,1,8,128]{3,2,0,1:T(8,128)(2,1)S(1)}, u32[]{:S(2)}, u32[]{:S(2)}) collective-permute-start(bf16[4,1,8,128]{3,2,0,1:T(8,128)(2,1)S(1)} %pad_maximum_fusion), channel_id=1, source_target_pairs={{4,0},{8,4},{12,8},{16,12},{20,16},{24,20},{28,24},{5,1},{9,5},{13... | collective-permute-start | bytes 24584 | tf_op jit(solution)/shard_map/ppermute | solution.py:41
  29.7 37.7 %copy-start.7 = (bf16[2,2,3]{2,1,0:T(2,128)(2,1)S(1)}, bf16[2,2,3]{2,1,0:T(2,128)(2,1)}, u32[]{:S(2)}) copy-start(bf16[2,2,3]{2,1,0:T(2,128)(2,1)} %get-tuple-element.33) | copy-start | bytes 76
  30.5 37.0 %copy-start.6 = (bf16[2,2,3]{2,1,0:T(2,128)(2,1)S(1)}, bf16[2,2,3]{2,1,0:T(2,128)(2,1)}, u32[]{:S(2)}) copy-start(bf16[2,2,3]{2,1,0:T(2,128)(2,1)} %get-tuple-element.32) | copy-start | bytes 76
  31.4 36.4 %copy-start.5 = (bf16[2,2,3]{2,1,0:T(2,128)(2,1)S(1)}, bf16[2,2,3]{2,1,0:T(2,128)(2,1)}, u32[]{:S(2)}) copy-start(bf16[2,2,3]{2,1,0:T(2,128)(2,1)} %get-tuple-element.31) | copy-start | bytes 76
  32.3 35.7 %copy-start.4 = (bf16[2,2,3]{2,1,0:T(2,128)(2,1)S(1)}, bf16[2,2,3]{2,1,0:T(2,128)(2,1)}, u32[]{:S(2)}) copy-start(bf16[2,2,3]{2,1,0:T(2,128)(2,1)} %get-tuple-element.30) | copy-start | bytes 76
  38.0 3.7 %collective-permute-start.7 = (bf16[2,1,2,128]{3,2,1,0:T(2,128)(2,1)S(1)}, bf16[2,1,2,128]{3,2,1,0:T(2,128)(2,1)S(1)}, u32[]{:S(2)}, u32[]{:S(2)}) collective-permute-start(bf16[2,1,2,128]{3,2,1,0:T(2,128)(2,1)S(1)} %get-tuple-element.13), channel_id=1, source_target_pairs={{0,1},{1,2},{2,3},{3,0},{4,5},{5,6},{6,7},{7,4},{8,9},{9,10},{10,1... | collective-permute-start | bytes 3080 | tf_op jit(solution)/shard_map/ppermute | solution.py:23
  38.1 3.6 %collective-permute-start.8 = (bf16[2,1,2,128]{3,2,1,0:T(2,128)(2,1)S(1)}, bf16[2,1,2,128]{3,2,1,0:T(2,128)(2,1)S(1)}, u32[]{:S(2)}, u32[]{:S(2)}) collective-permute-start(bf16[2,1,2,128]{3,2,1,0:T(2,128)(2,1)S(1)} %get-tuple-element.13), channel_id=1, source_target_pairs={{0,3},{1,0},{2,1},{3,2},{4,7},{5,4},{6,5},{7,6},{8,11},{9,8},{10,9... | collective-permute-start | bytes 3080 | tf_op jit(solution)/shard_map/ppermute | solution.py:26
  41.7 3.6 %collective-permute-start.9 = (bf16[2,1,2,128]{3,2,1,0:T(2,128)(2,1)S(1)}, bf16[2,1,2,128]{3,2,1,0:T(2,128)(2,1)S(1)}, u32[]{:S(2)}, u32[]{:S(2)}) collective-permute-start(bf16[2,1,2,128]{3,2,1,0:T(2,128)(2,1)S(1)} %collective-permute-done.7), channel_id=1, source_target_pairs={{0,1},{1,2},{2,3},{3,0},{4,5},{5,6},{6,7},{7,4},{8,9},{9,10},{10,1... | collective-permute-start | bytes 3080 | tf_op jit(solution)/shard_map/ppermute | solution.py:23
  45.5 11.6 %collective-permute-start.11 = (bf16[1,1,8,128]{3,2,1,0:T(8,128)(2,1)S(1)}, bf16[1,1,8,128]{3,2,1,0:T(8,128)(2,1)S(1)}, u32[]{:S(2)}, u32[]{:S(2)}) collective-permute-start(bf16[1,1,8,128]{3,2,1,0:T(8,128)(2,1)S(1)} %get-tuple-element.24), channel_id=1, source_target_pairs={{32,0},{64,32},{96,64},{128,96},{160,128},{192,160},{224,192},{33,... | collective-permute-start | bytes 6152 | tf_op jit(solution)/shard_map/ppermute | solution.py:41
  50.7 7.0 %collective-permute-start.10 = (bf16[1,1,8,128]{3,2,0,1:T(8,128)(2,1)S(1)}, bf16[1,1,8,128]{3,2,0,1:T(8,128)(2,1)S(1)}, u32[]{:S(2)}, u32[]{:S(2)}) collective-permute-start(bf16[1,1,8,128]{3,2,0,1:T(8,128)(2,1)S(1)} %get-tuple-element.23), channel_id=1, source_target_pairs={{0,32},{32,64},{64,96},{96,128},{128,160},{160,192},{192,224},{1,3... | collective-permute-start | bytes 6152 | tf_op jit(solution)/shard_map/ppermute | solution.py:39
  57.8 7.9 %collective-permute-start.12 = (bf16[4,1,8,128]{3,2,0,1:T(8,128)(2,1)S(1)}, bf16[4,1,8,128]{3,2,0,1:T(8,128)(2,1)S(1)}, u32[]{:S(2)}, u32[]{:S(2)}) collective-permute-start(bf16[4,1,8,128]{3,2,0,1:T(8,128)(2,1)S(1)} %pad_maximum_fusion.1), channel_id=1, source_target_pairs={{0,4},{4,8},{8,12},{12,16},{16,20},{20,24},{24,28},{1,5},{5,9},{9,... | collective-permute-start | bytes 24584 | tf_op jit(solution)/shard_map/ppermute | solution.py:39
  60.7 5.8 %collective-permute-start.13 = (bf16[4,1,8,128]{3,2,0,1:T(8,128)(2,1)S(1)}, bf16[4,1,8,128]{3,2,0,1:T(8,128)(2,1)S(1)}, u32[]{:S(2)}, u32[]{:S(2)}) collective-permute-start(bf16[4,1,8,128]{3,2,0,1:T(8,128)(2,1)S(1)} %pad_maximum_fusion.1), channel_id=1, source_target_pairs={{4,0},{8,4},{12,8},{16,12},{20,16},{24,20},{28,24},{5,1},{9,5},{13... | collective-permute-start | bytes 24584 | tf_op jit(solution)/shard_map/ppermute | solution.py:41
  69.5 3.7 %collective-permute-start.14 = (bf16[2,1,2,128]{3,2,1,0:T(2,128)(2,1)S(1)}, bf16[2,1,2,128]{3,2,1,0:T(2,128)(2,1)S(1)}, u32[]{:S(2)}, u32[]{:S(2)}) collective-permute-start(bf16[2,1,2,128]{3,2,1,0:T(2,128)(2,1)S(1)} %get-tuple-element.10), channel_id=1, source_target_pairs={{0,1},{1,2},{2,3},{3,0},{4,5},{5,6},{6,7},{7,4},{8,9},{9,10},{10,1... | collective-permute-start | bytes 3080 | tf_op jit(solution)/shard_map/ppermute | solution.py:23
  69.6 3.6 %collective-permute-start.15 = (bf16[2,1,2,128]{3,2,1,0:T(2,128)(2,1)S(1)}, bf16[2,1,2,128]{3,2,1,0:T(2,128)(2,1)S(1)}, u32[]{:S(2)}, u32[]{:S(2)}) collective-permute-start(bf16[2,1,2,128]{3,2,1,0:T(2,128)(2,1)S(1)} %get-tuple-element.10), channel_id=1, source_target_pairs={{0,3},{1,0},{2,1},{3,2},{4,7},{5,4},{6,5},{7,6},{8,11},{9,8},{10,9... | collective-permute-start | bytes 3080 | tf_op jit(solution)/shard_map/ppermute | solution.py:26
  73.2 3.6 %collective-permute-start.16 = (bf16[2,1,2,128]{3,2,1,0:T(2,128)(2,1)S(1)}, bf16[2,1,2,128]{3,2,1,0:T(2,128)(2,1)S(1)}, u32[]{:S(2)}, u32[]{:S(2)}) collective-permute-start(bf16[2,1,2,128]{3,2,1,0:T(2,128)(2,1)S(1)} %collective-permute-done.14), channel_id=1, source_target_pairs={{0,1},{1,2},{2,3},{3,0},{4,5},{5,6},{6,7},{7,4},{8,9},{9,10},{10,1... | collective-permute-start | bytes 3080 | tf_op jit(solution)/shard_map/ppermute | solution.py:23
  77.0 11.4 %collective-permute-start.18 = (bf16[1,1,8,128]{3,2,1,0:T(8,128)(2,1)S(1)}, bf16[1,1,8,128]{3,2,1,0:T(8,128)(2,1)S(1)}, u32[]{:S(2)}, u32[]{:S(2)}) collective-permute-start(bf16[1,1,8,128]{3,2,1,0:T(8,128)(2,1)S(1)} %get-tuple-element.22), channel_id=1, source_target_pairs={{32,0},{64,32},{96,64},{128,96},{160,128},{192,160},{224,192},{33,... | collective-permute-start | bytes 6152 | tf_op jit(solution)/shard_map/ppermute | solution.py:41
  80.8 8.3 %collective-permute-start.17 = (bf16[1,1,8,128]{3,2,0,1:T(8,128)(2,1)S(1)}, bf16[1,1,8,128]{3,2,0,1:T(8,128)(2,1)S(1)}, u32[]{:S(2)}, u32[]{:S(2)}) collective-permute-start(bf16[1,1,8,128]{3,2,0,1:T(8,128)(2,1)S(1)} %get-tuple-element.21), channel_id=1, source_target_pairs={{0,32},{32,64},{64,96},{96,128},{128,160},{160,192},{192,224},{1,3... | collective-permute-start | bytes 6152 | tf_op jit(solution)/shard_map/ppermute | solution.py:39
  89.1 7.9 %collective-permute-start.19 = (bf16[4,1,8,128]{3,2,0,1:T(8,128)(2,1)S(1)}, bf16[4,1,8,128]{3,2,0,1:T(8,128)(2,1)S(1)}, u32[]{:S(2)}, u32[]{:S(2)}) collective-permute-start(bf16[4,1,8,128]{3,2,0,1:T(8,128)(2,1)S(1)} %pad_maximum_fusion.2), channel_id=1, source_target_pairs={{0,4},{4,8},{8,12},{12,16},{16,20},{20,24},{24,28},{1,5},{5,9},{9,... | collective-permute-start | bytes 24584 | tf_op jit(solution)/shard_map/ppermute | solution.py:39
  91.2 6.6 %collective-permute-start.20 = (bf16[4,1,8,128]{3,2,0,1:T(8,128)(2,1)S(1)}, bf16[4,1,8,128]{3,2,0,1:T(8,128)(2,1)S(1)}, u32[]{:S(2)}, u32[]{:S(2)}) collective-permute-start(bf16[4,1,8,128]{3,2,0,1:T(8,128)(2,1)S(1)} %pad_maximum_fusion.2), channel_id=1, source_target_pairs={{4,0},{8,4},{12,8},{16,12},{20,16},{24,20},{28,24},{5,1},{9,5},{13... | collective-permute-start | bytes 24584 | tf_op jit(solution)/shard_map/ppermute | solution.py:41
  100.8 3.7 %collective-permute-start.21 = (bf16[2,1,2,128]{3,2,1,0:T(2,128)(2,1)S(1)}, bf16[2,1,2,128]{3,2,1,0:T(2,128)(2,1)S(1)}, u32[]{:S(2)}, u32[]{:S(2)}) collective-permute-start(bf16[2,1,2,128]{3,2,1,0:T(2,128)(2,1)S(1)} %get-tuple-element.6), channel_id=1, source_target_pairs={{0,1},{1,2},{2,3},{3,0},{4,5},{5,6},{6,7},{7,4},{8,9},{9,10},{10,1... | collective-permute-start | bytes 3080 | tf_op jit(solution)/shard_map/ppermute | solution.py:23
  100.9 3.6 %collective-permute-start.22 = (bf16[2,1,2,128]{3,2,1,0:T(2,128)(2,1)S(1)}, bf16[2,1,2,128]{3,2,1,0:T(2,128)(2,1)S(1)}, u32[]{:S(2)}, u32[]{:S(2)}) collective-permute-start(bf16[2,1,2,128]{3,2,1,0:T(2,128)(2,1)S(1)} %get-tuple-element.6), channel_id=1, source_target_pairs={{0,3},{1,0},{2,1},{3,2},{4,7},{5,4},{6,5},{7,6},{8,11},{9,8},{10,9... | collective-permute-start | bytes 3080 | tf_op jit(solution)/shard_map/ppermute | solution.py:26
  104.5 3.6 %collective-permute-start.23 = (bf16[2,1,2,128]{3,2,1,0:T(2,128)(2,1)S(1)}, bf16[2,1,2,128]{3,2,1,0:T(2,128)(2,1)S(1)}, u32[]{:S(2)}, u32[]{:S(2)}) collective-permute-start(bf16[2,1,2,128]{3,2,1,0:T(2,128)(2,1)S(1)} %collective-permute-done.21), channel_id=1, source_target_pairs={{0,1},{1,2},{2,3},{3,0},{4,5},{5,6},{6,7},{7,4},{8,9},{9,10},{10,1... | collective-permute-start | bytes 3080 | tf_op jit(solution)/shard_map/ppermute | solution.py:23
  108.3 11.4 %collective-permute-start.25 = (bf16[1,1,8,128]{3,2,1,0:T(8,128)(2,1)S(1)}, bf16[1,1,8,128]{3,2,1,0:T(8,128)(2,1)S(1)}, u32[]{:S(2)}, u32[]{:S(2)}) collective-permute-start(bf16[1,1,8,128]{3,2,1,0:T(8,128)(2,1)S(1)} %get-tuple-element.20), channel_id=1, source_target_pairs={{32,0},{64,32},{96,64},{128,96},{160,128},{192,160},{224,192},{33,... | collective-permute-start | bytes 6152 | tf_op jit(solution)/shard_map/ppermute | solution.py:41
  110.9 9.5 %collective-permute-start.24 = (bf16[1,1,8,128]{3,2,0,1:T(8,128)(2,1)S(1)}, bf16[1,1,8,128]{3,2,0,1:T(8,128)(2,1)S(1)}, u32[]{:S(2)}, u32[]{:S(2)}) collective-permute-start(bf16[1,1,8,128]{3,2,0,1:T(8,128)(2,1)S(1)} %get-tuple-element.19), channel_id=1, source_target_pairs={{0,32},{32,64},{64,96},{96,128},{128,160},{160,192},{192,224},{1,3... | collective-permute-start | bytes 6152 | tf_op jit(solution)/shard_map/ppermute | solution.py:39
  120.4 7.9 %collective-permute-start.26 = (bf16[4,1,8,128]{3,2,0,1:T(8,128)(2,1)S(1)}, bf16[4,1,8,128]{3,2,0,1:T(8,128)(2,1)S(1)}, u32[]{:S(2)}, u32[]{:S(2)}) collective-permute-start(bf16[4,1,8,128]{3,2,0,1:T(8,128)(2,1)S(1)} %pad_maximum_fusion.3), channel_id=1, source_target_pairs={{0,4},{4,8},{8,12},{12,16},{16,20},{20,24},{24,28},{1,5},{5,9},{9,... | collective-permute-start | bytes 24584 | tf_op jit(solution)/shard_map/ppermute | solution.py:39
  122.3 6.8 %collective-permute-start.27 = (bf16[4,1,8,128]{3,2,0,1:T(8,128)(2,1)S(1)}, bf16[4,1,8,128]{3,2,0,1:T(8,128)(2,1)S(1)}, u32[]{:S(2)}, u32[]{:S(2)}) collective-permute-start(bf16[4,1,8,128]{3,2,0,1:T(8,128)(2,1)S(1)} %pad_maximum_fusion.3), channel_id=1, source_target_pairs={{4,0},{8,4},{12,8},{16,12},{20,16},{24,20},{28,24},{5,1},{9,5},{13... | collective-permute-start | bytes 24584 | tf_op jit(solution)/shard_map/ppermute | solution.py:41
  132.0 31.3 %copy-start.2 = (f32[2,1,2,128]{3,2,1,0:T(2,128)S(1)}, f32[2,1,2,128]{3,2,1,0:T(2,128)}, u32[]{:S(2)}) copy-start(f32[2,1,2,128]{3,2,1,0:T(2,128)} %param.8) | copy-start | bytes 6148
  132.0 3.7 %collective-permute-start.28 = (bf16[2,1,2,128]{3,2,1,0:T(2,128)(2,1)S(1)}, bf16[2,1,2,128]{3,2,1,0:T(2,128)(2,1)S(1)}, u32[]{:S(2)}, u32[]{:S(2)}) collective-permute-start(bf16[2,1,2,128]{3,2,1,0:T(2,128)(2,1)S(1)} %get-tuple-element.3), channel_id=1, source_target_pairs={{0,1},{1,2},{2,3},{3,0},{4,5},{5,6},{6,7},{7,4},{8,9},{9,10},{10,1... | collective-permute-start | bytes 3080 | tf_op jit(solution)/shard_map/ppermute | solution.py:23
  132.1 3.6 %collective-permute-start.29 = (bf16[2,1,2,128]{3,2,1,0:T(2,128)(2,1)S(1)}, bf16[2,1,2,128]{3,2,1,0:T(2,128)(2,1)S(1)}, u32[]{:S(2)}, u32[]{:S(2)}) collective-permute-start(bf16[2,1,2,128]{3,2,1,0:T(2,128)(2,1)S(1)} %get-tuple-element.3), channel_id=1, source_target_pairs={{0,3},{1,0},{2,1},{3,2},{4,7},{5,4},{6,5},{7,6},{8,11},{9,8},{10,9... | collective-permute-start | bytes 3080 | tf_op jit(solution)/shard_map/ppermute | solution.py:26
  135.8 3.6 %collective-permute-start.30 = (bf16[2,1,2,128]{3,2,1,0:T(2,128)(2,1)S(1)}, bf16[2,1,2,128]{3,2,1,0:T(2,128)(2,1)S(1)}, u32[]{:S(2)}, u32[]{:S(2)}) collective-permute-start(bf16[2,1,2,128]{3,2,1,0:T(2,128)(2,1)S(1)} %collective-permute-done.28), channel_id=1, source_target_pairs={{0,1},{1,2},{2,3},{3,0},{4,5},{5,6},{6,7},{7,4},{8,9},{9,10},{10,1... | collective-permute-start | bytes 3080 | tf_op jit(solution)/shard_map/ppermute | solution.py:23
  139.5 11.4 %collective-permute-start.32 = (bf16[1,1,8,128]{3,2,1,0:T(8,128)(2,1)S(1)}, bf16[1,1,8,128]{3,2,1,0:T(8,128)(2,1)S(1)}, u32[]{:S(2)}, u32[]{:S(2)}) collective-permute-start(bf16[1,1,8,128]{3,2,1,0:T(8,128)(2,1)S(1)} %get-tuple-element.18), channel_id=1, source_target_pairs={{32,0},{64,32},{96,64},{128,96},{160,128},{192,160},{224,192},{33,... | collective-permute-start | bytes 6152 | tf_op jit(solution)/shard_map/ppermute | solution.py:41
  141.4 10.2 %collective-permute-start.31 = (bf16[1,1,8,128]{3,2,0,1:T(8,128)(2,1)S(1)}, bf16[1,1,8,128]{3,2,0,1:T(8,128)(2,1)S(1)}, u32[]{:S(2)}, u32[]{:S(2)}) collective-permute-start(bf16[1,1,8,128]{3,2,0,1:T(8,128)(2,1)S(1)} %get-tuple-element.17), channel_id=1, source_target_pairs={{0,32},{32,64},{64,96},{96,128},{128,160},{160,192},{192,224},{1,3... | collective-permute-start | bytes 6152 | tf_op jit(solution)/shard_map/ppermute | solution.py:39
  151.6 7.9 %collective-permute-start.33 = (bf16[4,1,8,128]{3,2,0,1:T(8,128)(2,1)S(1)}, bf16[4,1,8,128]{3,2,0,1:T(8,128)(2,1)S(1)}, u32[]{:S(2)}, u32[]{:S(2)}) collective-permute-start(bf16[4,1,8,128]{3,2,0,1:T(8,128)(2,1)S(1)} %pad_maximum_fusion.4), channel_id=1, source_target_pairs={{0,4},{4,8},{8,12},{12,16},{16,20},{20,24},{24,28},{1,5},{5,9},{9,... | collective-permute-start | bytes 24584 | tf_op jit(solution)/shard_map/ppermute | solution.py:39
  153.5 6.8 %collective-permute-start.34 = (bf16[4,1,8,128]{3,2,0,1:T(8,128)(2,1)S(1)}, bf16[4,1,8,128]{3,2,0,1:T(8,128)(2,1)S(1)}, u32[]{:S(2)}, u32[]{:S(2)}) collective-permute-start(bf16[4,1,8,128]{3,2,0,1:T(8,128)(2,1)S(1)} %pad_maximum_fusion.4), channel_id=1, source_target_pairs={{4,0},{8,4},{12,8},{16,12},{20,16},{24,20},{28,24},{5,1},{9,5},{13... | collective-permute-start | bytes 24584 | tf_op jit(solution)/shard_map/ppermute | solution.py:41
